TPU v7x, 256 devices: a whole 4x4x8 slice. The times are simulated.
256 devices in a mesh: pair: 8 (over x, y_lo), row: 32 (over y_hi, z, core).
Axes of the slice: x: 4, y: 4 (y_hi: 2, y_lo: 2; y = y_hi * 2 + y_lo), z: 8, core: 2. Of those that a mesh axis runs over, the one named last changes fastest.
Arguments:
- matrix: float32 [2, 131072, 1024], P(None, 'row', 'pair'), may hold values from -100 to 100, as said below
Outputs:
- rotated_matrix: float32 [2, 131072, 1024], P(None, 'row', 'pair')
Inputs may be any that keep to these rules, and one draw needn't show every extreme that they name: `matrix`: entries are real values with column blocks that are far from orthogonal to one another.
All inputs are finite; a program needn't handle non-finite values.
Results may differ from a plain program's by a relative error of at most 0.00014.
Values sent between devices are 32-bit elements; how exact they have to be, the bound alone decides.
A program may use at most 64 MiB of HBM per device.

v0:
```python
import jax
import jax.numpy as jnp
from jax import lax
from jax.sharding import PartitionSpec as P

STEPS = 2
SWEEPS = 2
NEWTON = 3


def shifted(block, axis, distance):
    devices = range(lax.axis_size(axis))
    route = [(i - distance, i) for i in devices if i - distance in devices]
    return lax.ppermute(block, axis, route)


def gram_of(left_cols, right_cols):
    return lax.dot_general(
        left_cols,
        right_cols,
        (((0,), (0,)), ((), ())),
        precision=lax.Precision.HIGHEST,
        preferred_element_type=jnp.float32,
    )


def product(left_mat, right_mat):
    return jnp.dot(
        left_mat, right_mat, precision=lax.Precision.HIGHEST, preferred_element_type=jnp.float32
    )


def polar_turn(gram_matrix):
    half_width = gram_matrix.shape[0] // 2
    diagonal = jnp.diagonal(gram_matrix)
    inverse = 1.0 / jnp.sqrt(diagonal + 1e-06)
    cross_part = (
        gram_matrix[:half_width, half_width:]
        * inverse[:half_width, None]
        * inverse[None, half_width:]
    )
    cross_part = cross_part / (1.0 + jnp.sqrt(jnp.sum(cross_part * cross_part)))
    zero_block = jnp.zeros((half_width, half_width), jnp.float32)
    skew_part = jnp.concatenate(
        [
            jnp.concatenate([zero_block, cross_part], 1),
            jnp.concatenate([-cross_part.T, zero_block], 1),
        ],
        0,
    )
    identity = jnp.eye(2 * half_width, dtype=jnp.float32)
    factor = identity + skew_part
    for repeat in range(NEWTON):
        factor = product(factor, 1.5 * identity - 0.5 * gram_of(factor, factor))
    return factor


def pair_rotation(gram_matrix):
    rotation = jnp.eye(gram_matrix.shape[0], dtype=jnp.float32)
    current = gram_matrix
    for sweep_index in range(SWEEPS):
        factor = polar_turn(current)
        rotation = product(rotation, factor)
        if sweep_index + 1 < SWEEPS:
            current = gram_of(factor, product(current, factor))
    return (rotation, current)


def plain_move(upper_block, lower_block):
    pairs_count = lax.axis_size("pair")
    position = lax.axis_index("pair")
    outgoing = jnp.where(position == 0, lower_block, upper_block)
    arrived = shifted(outgoing, "pair", 1)
    below = shifted(lower_block, "pair", -1)
    new_upper = jnp.where(position == 0, upper_block, arrived)
    new_lower = jnp.where(position == pairs_count - 1, upper_block, below)
    return (new_upper, new_lower)


def body(matrix):
    upper_block = matrix[0]
    lower_block = matrix[1]
    half_width = upper_block.shape[1]
    for step_index in range(STEPS):
        pair_cols = jnp.concatenate([upper_block, lower_block], 1)
        gram_matrix = lax.psum(gram_of(pair_cols, pair_cols), "row")
        rotation, current = pair_rotation(gram_matrix)
        rotated = product(pair_cols, rotation)
        upper_block = rotated[:, :half_width]
        lower_block = rotated[:, half_width:]
        upper_block, lower_block = plain_move(upper_block, lower_block)
    return jnp.stack([upper_block, lower_block], 0)


def solution(mesh):
    in_specs = (P(None, "row", "pair"),)
    out_specs = P(None, "row", "pair")
    return jax.shard_map(body, mesh=mesh, in_specs=in_specs, out_specs=out_specs, check_vma=False)
```

profile of v0, /device:TPU:1, one launch (start us, length us, event | category | flops | bytes accessed | tf_op | source)
XLA Modules:
  0.0 803.5 jit_solution(11936363470819997771)
XLA Ops:
  6.5 2.5 slice_bitcast_fusion.1
  9.0 1.3 copy-done.1
  10.4 7.7 fusion.3
  18.5 267.4 %all-reduce.11.cloned.1.call-done = f32[256,256]{1,0:T(8,128)} async-done(((f32[256,256]{1,0:T(8,128)}), f32[256,256]{1,0:T(8,128)}) %all-reduce.11.cloned.1.call-update) | async-done | bytes 262160 | tf_op jit(solution)/shard_map/psum | solution.py:86
  285.9 2.6 gather_fusion
  288.5 1.6 multiply_reduce_fusion.3
  290.7 0.9 negate_bitcast_fusion.3
  296.1 2.9 gather_fusion.1
  299.0 0.7 multiply_reduce_fusion.2
  302.4 0.6 select_subtract_fusion.6
  303.9 4.3 fusion.2
  308.2 2.4 slice_select_fusion.3
  310.6 0.8 copy-done
  311.4 2.3 collective-permute-start
  313.8 1.5 collective-permute-start.1
  315.2 88.0 %collective-permute-done = f32[4096,128]{0,1:T(8,128)S(1)} collective-permute-done((f32[4096,128]{0,1:T(8,128)}, f32[4096,128]{0,1:T(8,128)S(1)}, u32[]{:S(2)}, u32[]{:S(2)}) %collective-permute-start) | collective-permute-done | bytes 2097184 | tf_op jit(solution)/shard_map/ppermute | solution.py:14
  403.3 1.3 copy-done.7
  404.6 2.6 slice_select_fusion.2
  407.3 1.3 copy-done.3
  408.6 4.2 fusion.1
  412.8 261.4 %all-reduce.13.cloned.1.call-done = f32[256,256]{1,0:T(8,128)} async-done(((f32[256,256]{1,0:T(8,128)}), f32[256,256]{1,0:T(8,128)}) %all-reduce.13.cloned.1.call-update) | async-done | bytes 262160 | tf_op jit(solution)/shard_map/psum | solution.py:86
  674.2 2.6 gather_fusion.2
  676.8 1.6 multiply_reduce_fusion.1
  679.0 0.9 negate_bitcast_fusion.1
  684.4 2.6 gather_fusion.3
  687.0 0.7 multiply_reduce_fusion
  691.9 4.1 fusion
  696.4 2.3 collective-permute-start.2
  698.8 1.3 collective-permute-start.3
  700.1 87.9 %collective-permute-done.2 = f32[4096,128]{0,1:T(8,128)S(1)} collective-permute-done((f32[4096,128]{0,1:T(8,128)S(1)}, f32[4096,128]{0,1:T(8,128)S(1)}, u32[]{:S(2)}, u32[]{:S(2)}) %collective-permute-start.2) | collective-permute-done | bytes 2097184 | tf_op jit(solution)/shard_map/ppermute | solution.py:14
  788.5 2.4 pad_maximum_fusion.2
  790.9 5.6 copy.15
  (66 shorter events, 16.5 us)
Async XLA Ops:
  6.5 279.4 %all-reduce.11.cloned.1.call-start = ((), (), s32[]{:S(2)}) async-start(), calls=%async_computation | async-start | bytes 524288 | tf_op jit(solution)/shard_map/psum | solution.py:86
  9.0 1.3 copy-start.1
  18.1 656.1 %all-reduce.13.cloned.1.call-start = ((), (), s32[]{:S(2)}) async-start(), calls=%async_computation.1 | async-start | bytes 524288 | tf_op jit(solution)/shard_map/psum | solution.py:86
  292.2 2.9 copy-start.5
  301.4 2.4 copy-start.2
  308.1 3.3 copy-start
  311.4 91.9 %collective-permute-start = (f32[4096,128]{0,1:T(8,128)}, f32[4096,128]{0,1:T(8,128)S(1)}, u32[]{:S(2)}, u32[]{:S(2)}) collective-permute-start(f32[4096,128]{0,1:T(8,128)} %get-tuple-element.19), channel_id=1, source_target_pairs={{0,32},{32,64},{64,96},{96,128},{128,160},{160,192},{192,224},{1,3... | collective-permute-start | bytes 6291464 | tf_op jit(solution)/shard_map/ppermute | solution.py:14
  313.8 90.8 %collective-permute-start.1 = (f32[4096,128]{0,1:T(8,128)}, f32[4096,128]{0,1:T(8,128)}, u32[]{:S(2)}, u32[]{:S(2)}) collective-permute-start(f32[4096,128]{0,1:T(8,128)} %get-tuple-element.20), channel_id=1, source_target_pairs={{32,0},{64,32},{96,64},{128,96},{160,128},{192,160},{224,192},{33,... | collective-permute-start | bytes 6291464 | tf_op jit(solution)/shard_map/ppermute | solution.py:14
  403.3 1.3 copy-start.7
  407.2 1.3 copy-start.3
  680.5 2.9 copy-start.6
  689.4 2.4 copy-start.4
  696.4 91.5 %collective-permute-start.2 = (f32[4096,128]{0,1:T(8,128)S(1)}, f32[4096,128]{0,1:T(8,128)S(1)}, u32[]{:S(2)}, u32[]{:S(2)}) collective-permute-start(f32[4096,128]{0,1:T(8,128)S(1)} %get-tuple-element.15), channel_id=1, source_target_pairs={{0,32},{32,64},{64,96},{96,128},{128,160},{160,192},{192,224},{1,3... | collective-permute-start | bytes 6291464 | tf_op jit(solution)/shard_map/ppermute | solution.py:14
  698.8 89.2 %collective-permute-start.3 = (f32[4096,128]{0,1:T(8,128)S(1)}, f32[4096,128]{0,1:T(8,128)S(1)}, u32[]{:S(2)}, u32[]{:S(2)}) collective-permute-start(f32[4096,128]{0,1:T(8,128)S(1)} %get-tuple-element.16), channel_id=1, source_target_pairs={{32,0},{64,32},{96,64},{128,96},{160,128},{192,160},{224,192},{33,... | collective-permute-start | bytes 6291464 | tf_op jit(solution)/shard_map/ppermute | solution.py:14
Sparse Core Ops, SparseCore 0:
  18.2 267.6 all-reduce.10
  413.0 261.2 all-reduce.12
where the time goes:
time: 812 us; the launch traced here: 804 us
  waiting for transfers between devices  705 us (87%)
  matrix products  35.4 us (4%)
  local copies, waits for them, and re-layouts  23.8 us (3%)
  between operations  16.7 us (2%)
  other arithmetic  15 us (2%)
    psum x2, waiting for transfers between devices, body(): gram_matrix = lax.psum(gram_of(pair_cols, pair_cols), 'row')  529 us
    ppermute x4, waiting for transfers between devices, shifted(): return lax.ppermute(block, axis, route)  176 us
    dot_general x16, matrix products, gram_of(): lax.dot_general(left_cols, right_cols, (((0,), (0,)), ((), ())), precisio...  19.7 us
  transfers between devices with their start and end apart: 6, of which 4 were waited for; matrix products, arithmetic and copies ran while one was open for 0% of the time, Pallas kernels for 0%

commit v1 on v0

v1 whole, which is shorter than its diff:
```python
import functools
import jax
import jax.numpy as jnp
from jax import lax
from jax.experimental import pallas as pl
from jax.experimental.pallas import tpu as pltpu
from jax.sharding import PartitionSpec as P

SWEEPS = 2
BW = 128
CHUNK = 512
MESH = pl.DeviceIdType.MESH
F32 = jnp.float32
BF16 = jnp.bfloat16

CHIPS = [(a, d) for d in (4, 3, 5, 2, 6, 1, 7, 0) for a in (1, 0) if (a, d) != (0, 0)]


def split(x):
    high = x.astype(BF16)
    return high, (x - high.astype(F32)).astype(BF16)


def mul(a, b, dims):
    return lax.dot_general(a, b, (dims, ((), ())), preferred_element_type=F32)


def mul3(a, b, dims=((1,), (0,))):
    ah, al = split(a)
    bh, bl = split(b)
    return mul(ah, bh, dims) + (mul(ah, bl, dims) + mul(al, bh, dims))


def mul6(a, b, dims=((1,), (0,))):
    return lax.dot_general(
        a, b, (dims, ((), ())), precision=lax.Precision.HIGHEST, preferred_element_type=F32
    )


small = mul6


def diag_mask():
    i = lax.broadcasted_iota(jnp.int32, (BW, BW), 0)
    j = lax.broadcasted_iota(jnp.int32, (BW, BW), 1)
    return i, j


def polar_even(t, eye):
    t2 = small(t, t)
    t3 = small(t2, t)
    t4 = small(t2, t2)
    e = 0.25 * t3 - 0.75 * t2
    m = eye - 0.5 * t + 0.375 * t2 - 0.3125 * t3 + 0.0625 * t4
    s = small(e, e)
    r = small(m, 0.375 * eye - 0.125 * e)
    return m + small(r, s)


def turn(cross, first_diag, second_diag, eye):
    c = cross * (1.0 / jnp.sqrt(first_diag + 1e-06)) * (1.0 / jnp.sqrt(second_diag + 1e-06))
    total = jnp.sum(jnp.sum(c * c, axis=1, keepdims=True), axis=0, keepdims=True)
    x = c / (1.0 + jnp.sqrt(total))
    xt = x.T
    a = polar_even(small(x, xt), eye)
    d = polar_even(small(xt, x), eye)
    b = small(a, x)
    return a, b, d


def whole(a, b, d):
    return jnp.concatenate(
        [jnp.concatenate([a, b], 1), jnp.concatenate([-b.T, d], 1)], 0
    )


def rotation(first, second, cross, first_diag, second_diag):
    i, j = diag_mask()
    eye = jnp.where(i == j, 1.0, 0.0).astype(F32)
    h = jnp.concatenate(
        [jnp.concatenate([first, cross], 1), jnp.concatenate([cross.T, second], 1)], 0
    )
    a, b, d = turn(cross, first_diag, second_diag, eye)
    y = whole(a, b, d)
    hy = small(h, y)
    new_cross = small(jnp.concatenate([a, -b], 1), hy[:, BW:])
    diag = jnp.sum(y * hy, axis=0, keepdims=True)
    new_first = jnp.sum(jnp.where(i == j, diag[:, :BW], 0.0), axis=1, keepdims=True)
    a, b, d = turn(new_cross, new_first, diag[:, BW:], eye)
    return h, small(y, whole(a, b, d))


def kernel(
    x_hbm, o_hbm,
    xin, xhi, xlo, own, far, out,
    pay, cbuf, dl, dlr, rsrc, rbuf, res, full, wbuf,
    gown, gfar, pay2, cbuf2, acc2, rbuf2, xsrc, xbuf, res2, full2,
    lsem, osem, cs, cr, rs_s, rs_r, ag_s, ag_r, fs, fr,
    ss, sr, gs, gr, cs2, cr2, rs2_s, rs2_r, xs, xr, ag2_s, ag2_r, fs2, fr2,
):
    p = lax.axis_index("pair")
    r = lax.axis_index("row")
    yh, z, c = r // 16, lax.rem(r // 2, 8), lax.rem(r, 2)
    chip = yh * 8 + z
    m = p // 2
    uc = lax.rem(m + 1, 2)
    half = lax.rem(m + p, 2)
    pu = jnp.where(p >= 2, p - 2, 1 - p)
    po = jnp.where(p <= 5, p + 2, 13 - p)
    partner = [jnp.where(uc == s, pu, po) for s in (0, 1)]
    mine = [jnp.where(uc == s, p == 0, p <= 6) for s in (0, 1)]
    lead = [jnp.where(uc == s, p != 1, p == 7) for s in (0, 1)]
    swap = jnp.logical_or(lax.rem(m, 2) == 1, p == 0)
    rows = x_hbm.shape[1]
    n_chunks = rows // CHUNK
    part = n_chunks // 2

    def chip_row(op, core):
        return lax.rem(yh + op[0], 2) * 16 + lax.rem(z + op[1], 8) * 2 + core

    def chip_index(op):
        return lax.rem(yh + op[0], 2) * 8 + lax.rem(z + op[1], 8)

    sibling = (p, chip_row((0, 0), 1 - c))
    peers = [(p, chip_row(op, c)) for op in CHIPS]

    def remote(src, dst, send, recv, device):
        return pltpu.make_async_remote_copy(
            src_ref=src, dst_ref=dst, send_sem=send, recv_sem=recv,
            device_id=device, device_id_type=MESH,
        )

    def load(k):
        return pltpu.make_async_copy(
            x_hbm.at[:, pl.ds(k * CHUNK, CHUNK)], xin.at[:, pl.ds(k * CHUNK, CHUNK)], lsem.at[k]
        )

    for k in range(n_chunks):
        load(k).start()
    barrier = pltpu.get_barrier_semaphore()
    everyone = [sibling] + peers + [(partner[0], r), (partner[1], r)]
    for device in everyone:
        pl.semaphore_signal(barrier, inc=1, device_id=device, device_id_type=MESH)

    def gram_chunk(k, g):
        load(k).wait()
        at = pl.ds(pl.multiple_of(k * CHUNK, CHUNK), CHUNK)
        high, low = split(jnp.concatenate([xin[0, at], xin[1, at]], 1))
        xhi[at] = high
        xlo[at] = low
        return g + mul(high, jnp.concatenate([high, low], 1), ((0,), (0,)))

    g = lax.fori_loop(0, n_chunks, gram_chunk, jnp.zeros((2 * BW, 4 * BW), F32))
    gl = g[:, 2 * BW:]
    g = g[:, :2 * BW] + (gl + gl.T)
    i, j = diag_mask()
    pay[0] = g[:BW, BW:]
    pay[1] = jnp.where(i >= j, g[:BW, :BW], g[BW:, BW:])
    low_diag = jnp.sum(jnp.where(i == j, g[BW:, BW:], 0.0), axis=0, keepdims=True)
    dl[...] = jnp.broadcast_to(low_diag, (8, BW))
    pl.semaphore_wait(barrier, len(everyone))

    c1 = remote(pay.at[1 - c], cbuf, cs.at[0], cr.at[0], sibling)
    c2 = remote(dl, dlr, cs.at[1], cr.at[1], sibling)
    c1.start()
    c2.start()
    c1.wait()
    c2.wait()
    rsrc[:, :8] = (pay[c] + cbuf[...]).reshape(16, 8, BW)
    rsrc[:, 8:] = jnp.broadcast_to((dl[...] + dlr[...])[None], (16, 8, BW))
    copies = []
    for n, op in enumerate(CHIPS):
        cp = remote(rsrc.at[chip_index(op)], rbuf.at[n], rs_s.at[n], rs_r.at[n], peers[n])
        cp.start()
        copies.append(cp)
    for cp in copies:
        cp.wait()
    total = rsrc[chip] + jnp.sum(rbuf[...], axis=0)
    low_diag = total[8:9]
    here = pl.ds(pl.multiple_of(chip * 8, 8), 8)
    res[here] = total[:8]
    copies = []
    for n, op in enumerate(CHIPS):
        cp = remote(res.at[here], res.at[here], ag_s.at[n], ag_r.at[n], peers[n])
        cp.start()
        copies.append(cp)
    for cp in copies:
        cp.wait()
    cp = remote(res, full.at[c], fs, fr, sibling)
    cp.start()
    full[c] = res[...]
    cp.wait()
    cross = full[0]
    packed = full[1]
    flipped = packed.T
    upper = jnp.where(i >= j, packed, flipped)
    lower = jnp.where(i == j, jnp.broadcast_to(low_diag, (BW, BW)), jnp.where(i < j, packed, flipped))
    up_diag = jnp.sum(jnp.where(i == j, upper, 0.0), axis=1, keepdims=True)
    h, v = rotation(upper, lower, cross, up_diag, low_diag)
    w = jnp.where(swap, jnp.concatenate([v[:, BW:], v[:, :BW]], 1), v)
    wh, wl = split(w)
    wbuf[0] = wh
    wbuf[1] = wl

    def send(k, s):
        at = pl.ds(pl.multiple_of(k * CHUNK, CHUNK), CHUNK)
        return remote(own.at[s, at], far.at[s, at], ss.at[s, k], sr.at[s, k], (partner[s], r))

    def product(k):
        at = pl.ds(pl.multiple_of(k * CHUNK, CHUNK), CHUNK)
        xh = xhi[at]
        dims = ((1,), (0,))
        y = mul(xh, wbuf[0], dims) + (mul(xh, wbuf[1], dims) + mul(xlo[at], wbuf[0], dims))
        own[0, at] = y[:, :BW]
        own[1, at] = y[:, BW:]

    def first_part(n, carry):
        k = half * part + n
        product(k)
        send(k, 0).start()
        send(k, 1).start()
        return carry

    lax.fori_loop(0, part, first_part, 0)

    hw = small(h, w)
    for s in (0, 1):
        gown[s] = small(w[:, s * BW:(s + 1) * BW].T, hw[:, s * BW:(s + 1) * BW])
    grams = [remote(gown.at[s], gfar.at[s], gs.at[s], gr.at[s], (partner[s], r)) for s in (0, 1)]
    for cp in grams:
        cp.start()

    def second_product(n, carry):
        product((1 - half) * part + n)
        return carry

    lax.fori_loop(0, part, second_product, 0)

    def cross_chunk(n, acc):
        k = (1 - half) * part + n
        at = pl.ds(pl.multiple_of(k * CHUNK, CHUNK), CHUNK)
        out_acc = []
        for s in (0, 1):
            send(k, s).wait_recv()
            lh, ll = split(own[s, at])
            fh, fl = split(far[s, at])
            dims = ((0,), (0,))
            q = mul(lh, jnp.concatenate([fh, fl], 1), dims)
            out_acc.append(acc[s] + (q[:, :BW] + (q[:, BW:] + mul(ll, fh, dims))))
        return tuple(out_acc)

    zero = jnp.zeros((BW, BW), F32)
    acc = lax.fori_loop(0, part, cross_chunk, (zero, zero))

    def second_send(n, carry):
        send(half * part + n, 0).wait_send()
        send(half * part + n, 1).wait_send()
        return carry

    lax.fori_loop(0, part, second_send, 0)
    for s in (0, 1):
        pay2[s] = jnp.where(mine[s], acc[s], acc[s].T)
    cp = remote(pay2.at[1 - c], cbuf2, cs2, cr2, sibling)
    cp.start()

    def second_start(n, carry):
        k = (1 - half) * part + n
        send(k, 0).start()
        send(k, 1).start()
        return carry

    lax.fori_loop(0, part, second_start, 0)
    cp.wait()
    acc2[...] = pay2[c] + cbuf2[...]
    copies = []
    for n, op in enumerate(CHIPS):
        at = pl.ds(pl.multiple_of(chip_index(op) * 8, 8), 8)
        cp = remote(acc2.at[at], rbuf2.at[n], rs2_s.at[n], rs2_r.at[n], peers[n])
        cp.start()
        copies.append(cp)
    for cp in copies:
        cp.wait()
    xsrc[...] = acc2[here] + jnp.sum(rbuf2[...], axis=0)
    edge = jnp.where(c == 0, partner[0], partner[1])
    cp = remote(xsrc, xbuf, xs, xr, (edge, r))
    cp.start()
    cp.wait()
    res2[here] = xsrc[...] + xbuf[...]
    copies = []
    for n, op in enumerate(CHIPS):
        cp = remote(res2.at[here], res2.at[here], ag2_s.at[n], ag2_r.at[n], peers[n])
        cp.start()
        copies.append(cp)
    for cp in copies:
        cp.wait()
    cp = remote(res2, full2.at[c], fs2, fr2, sibling)
    cp.start()
    full2[c] = res2[...]
    for q in grams:
        q.wait()
    cp.wait()

    weights = []
    for s in (0, 1):
        first = jnp.where(mine[s], gown[s], gfar[s])
        second = jnp.where(mine[s], gfar[s], gown[s])
        fd = jnp.sum(jnp.where(i == j, first, 0.0), axis=1, keepdims=True)
        sd = jnp.sum(jnp.where(i == j, second, 0.0), axis=0, keepdims=True)
        _, v = rotation(first, second, full2[s], fd, sd)
        v = jnp.where(lead[s], v[:, :BW], v[:, BW:])
        v = jnp.where(mine[s], v, jnp.concatenate([v[BW:], v[:BW]], 0))
        weights.append(split(v))

    def store(k, s):
        at = pl.ds(pl.multiple_of(k * CHUNK, CHUNK), CHUNK)
        slot = jnp.where(uc == s, 0, 1)
        return pltpu.make_async_copy(out.at[s, at], o_hbm.at[slot, at], osem.at[s, k])

    def last_product(k):
        at = pl.ds(pl.multiple_of(k * CHUNK, CHUNK), CHUNK)
        dims = ((1,), (0,))
        for s in (0, 1):
            vh, vl = weights[s]
            bh, bl = split(jnp.concatenate([own[s, at], far[s, at]], 1))
            out[s, at] = mul(bh, vh, dims) + (mul(bh, vl, dims) + mul(bl, vh, dims))
            store(k, s).start()

    def last_a(n, carry):
        last_product((1 - half) * part + n)
        return carry

    lax.fori_loop(0, part, last_a, 0)

    def last_b(n, carry):
        k = half * part + n
        send(k, 0).wait_recv()
        send(k, 1).wait_recv()
        last_product(k)
        return carry

    lax.fori_loop(0, part, last_b, 0)

    def finish(k, carry):
        store(k, 0).wait()
        store(k, 1).wait()
        return carry

    lax.fori_loop(0, n_chunks, finish, 0)

    def finish_send(n, carry):
        k = (1 - half) * part + n
        send(k, 0).wait_send()
        send(k, 1).wait_send()
        return carry

    lax.fori_loop(0, part, finish_send, 0)


def body(matrix):
    rows = matrix.shape[1]
    n_chunks = rows // CHUNK
    dma = pltpu.SemaphoreType.DMA
    n = len(CHIPS)
    block = pltpu.VMEM((2, rows, BW), F32)
    square = pltpu.VMEM((BW, BW), F32)
    squares = pltpu.VMEM((2, BW, BW), F32)
    tile = pltpu.VMEM((8, BW), F32)
    scratch = [
        block, pltpu.VMEM((rows, 2 * BW), BF16), pltpu.VMEM((rows, 2 * BW), BF16), block, block, block,
        squares, square, tile, tile, pltpu.VMEM((16, 16, BW), F32), pltpu.VMEM((n, 16, BW), F32),
        square, squares, pltpu.VMEM((2, 2 * BW, 2 * BW), BF16),
        squares, squares, squares, square, square, pltpu.VMEM((n, 8, BW), F32), tile, tile, square, squares,
        dma((n_chunks,)), dma((2, n_chunks)), dma((2,)), dma((2,)), dma((n,)), dma((n,)), dma((n,)), dma((n,)),
        dma, dma, dma((2, n_chunks)), dma((2, n_chunks)), dma((2,)), dma((2,)), dma, dma, dma((n,)), dma((n,)),
        dma, dma, dma((n,)), dma((n,)), dma, dma,
    ]
    return pl.pallas_call(
        kernel,
        out_shape=jax.ShapeDtypeStruct(matrix.shape, F32),
        in_specs=[pl.BlockSpec(memory_space=pl.ANY)],
        out_specs=pl.BlockSpec(memory_space=pl.ANY),
        scratch_shapes=scratch,
        compiler_params=pltpu.CompilerParams(
            collective_id=0, has_side_effects=True, vmem_limit_bytes=48 << 20
        ),
    )(matrix)


def solution(mesh):
    specs = P(None, "row", "pair")
    return jax.shard_map(body, mesh=mesh, in_specs=(specs,), out_specs=specs, check_vma=False)
```

time: 812 us -> 114 us (0.14); the launches traced: 804 us -> 114 us
  waiting for transfers between devices: 705 us -> 0 us
  Pallas kernels: 0 us -> 112 us
  matrix products: 35.4 us -> 0 us
  local copies, waits for them, and re-layouts: 23.8 us -> 2.02 us
  between operations: 16.7 us -> 0.01 us
  other arithmetic: 15 us -> 0 us
    psum x2 -> x0, waiting for transfers between devices: 529 us -> none  [body(): gram_matrix = lax.psum(gram_of(pair_cols, pair_cols), 'row')]
    ppermute x4 -> x0, waiting for transfers between devices: 176 us -> none  [shifted(): return lax.ppermute(block, axis, route)]
    pallas_call x0 -> x1, Pallas kernels: none -> 112 us  [body(): pl.pallas_call(kernel, out_shape=jax.ShapeDtypeStruct(matrix.shape, F32),...]
    dot_general x36 -> x0, matrix products: 35.4 us -> none  [the longest x16 19.7 us: gram_of(): lax.dot_general(left_cols, right_cols, (((0,), (0,)), ((), ())), precisio...]
    gather x4 -> x0, local copies, waits for them, and re-layouts: 10.6 us -> none  [polar_turn(): diagonal = jnp.diagonal(gram_matrix)]
  transfers between devices with their start and end apart: 6 -> 0, of which waited for: 4 -> 0; matrix products, arithmetic and copies ran while one was open for 0% -> 0% of each run, Pallas kernels for 0% -> 0%
where the time goes in v1:
time: 114 us
  Pallas kernels  112 us (98%)
  local copies, waits for them, and re-layouts  2.02 us (2%)
    pallas_call x1, Pallas kernels, body(): pl.pallas_call(kernel, out_shape=jax.ShapeDtypeStruct(matrix.shape, F32),...  112 us

profile of v1, /device:TPU:1, one launch (start us, length us, event | category | flops | bytes accessed | tf_op | source)
XLA Modules:
  0.0 114.2 jit_solution(4102979872599437863)
XLA Ops:
  0.0 112.2 %shard_map.17 = f32[2,4096,128]{2,1,0:T(8,128)S(1)} custom-call(f32[2,4096,128]{2,1,0:T(8,128)} %x_hbm.1), custom_call_target="tpu_custom_call" | custom-call | tf_op jit(solution)/shard_map/pallas_call | solution.py:377
  112.2 2.0 %copy.3 = f32[2,4096,128]{2,1,0:T(8,128)} copy(f32[2,4096,128]{2,1,0:T(8,128)S(1)} %shard_map.17) | data formatting | bytes 8388608

commit v2 on v1

v2 whole, which is shorter than its diff:
```python
import functools
import jax
import jax.numpy as jnp
from jax import lax
from jax.experimental import pallas as pl
from jax.experimental.pallas import tpu as pltpu
from jax.sharding import PartitionSpec as P

SWEEPS = 2
BW = 128
CHUNK = 256
EARLY = 3
PACE = (1, 2, 2, 3)
LAST = 2
MESH = pl.DeviceIdType.MESH
F32 = jnp.float32
BF16 = jnp.bfloat16

CHIPS = [(a, d) for d in (4, 3, 5, 2, 6, 1, 7, 0) for a in (1, 0) if (a, d) != (0, 0)]


def split(x):
    high = x.astype(BF16)
    return high, (x - high.astype(F32)).astype(BF16)


def mul(a, b, dims):
    return lax.dot_general(a, b, (dims, ((), ())), preferred_element_type=F32)


def mul3(a, b, dims=((1,), (0,))):
    ah, al = split(a)
    bh, bl = split(b)
    return mul(ah, bh, dims) + (mul(ah, bl, dims) + mul(al, bh, dims))


def mul6(a, b, dims=((1,), (0,))):
    return lax.dot_general(
        a, b, (dims, ((), ())), precision=lax.Precision.HIGHEST, preferred_element_type=F32
    )


small = mul6


def diag_mask():
    i = lax.broadcasted_iota(jnp.int32, (BW, BW), 0)
    j = lax.broadcasted_iota(jnp.int32, (BW, BW), 1)
    return i, j


def polar_even(ts, eye):
    t2 = [small(t, t) for t in ts]
    t3 = [small(u, t) for u, t in zip(t2, ts)]
    t4 = [small(u, u) for u in t2]
    e = [0.25 * w - 0.75 * u for w, u in zip(t3, t2)]
    m = [
        eye - 0.5 * t + 0.375 * u - 0.3125 * w + 0.0625 * q
        for t, u, w, q in zip(ts, t2, t3, t4)
    ]
    s = [small(u, u) for u in e]
    r = [small(w, 0.375 * eye - 0.125 * u) for w, u in zip(m, e)]
    return [w + small(u, q) for w, u, q in zip(m, r, s)]


def turn(items, eye):
    cs = [
        cross * (1.0 / jnp.sqrt(fd + 1e-06)) * (1.0 / jnp.sqrt(sd + 1e-06))
        for cross, fd, sd in items
    ]
    totals = [jnp.sum(jnp.sum(c * c, axis=1, keepdims=True), axis=0, keepdims=True) for c in cs]
    xs = [c / (1.0 + jnp.sqrt(total)) for c, total in zip(cs, totals)]
    xts = [x.T for x in xs]
    ts = [small(x, xt) for x, xt in zip(xs, xts)] + [small(xt, x) for x, xt in zip(xs, xts)]
    evens = polar_even(ts, eye)
    n = len(items)
    return [(evens[k], small(evens[k], xs[k]), evens[n + k]) for k in range(n)]


def whole(a, b, d):
    return jnp.concatenate([jnp.concatenate([a, b], 1), jnp.concatenate([-b.T, d], 1)], 0)


def rotations(items):
    i, j = diag_mask()
    eye = jnp.where(i == j, 1.0, 0.0).astype(F32)
    hs = [
        jnp.concatenate([jnp.concatenate([f, c], 1), jnp.concatenate([c.T, s], 1)], 0)
        for f, s, c, _, _ in items
    ]
    turns = turn([item[2:] for item in items], eye)
    ys = [whole(*t) for t in turns]
    hys = [small(h, y) for h, y in zip(hs, ys)]
    crosses = [
        small(jnp.concatenate([a, -b], 1), hy[:, BW:]) for (a, b, _), hy in zip(turns, hys)
    ]
    diags = [jnp.sum(y * hy, axis=0, keepdims=True) for y, hy in zip(ys, hys)]
    firsts = [
        jnp.sum(jnp.where(i == j, diag[:, :BW], 0.0), axis=1, keepdims=True) for diag in diags
    ]
    turns = turn(
        [(c, f, diag[:, BW:]) for c, f, diag in zip(crosses, firsts, diags)], eye
    )
    return [(h, small(y, whole(*t))) for h, y, t in zip(hs, ys, turns)]


def kernel(
    x_hbm, o_hbm,
    xin, xhi, xlo, own, far, out, bhi, blo,
    pay, cbuf, dl, dlr, rsrc, rbuf, res, full, wbuf,
    ebuf, wown, wfar, gown, gfar, pay2, cbuf2, acc2, rbuf2, res2, full2,
    lsem, osem, cs, cr, rs_s, rs_r, ag_s, ag_r, fs, fr,
    es, er, ws, wr, ss, sr, gs, gr, cs2, cr2, rs2_s, rs2_r, ag2_s, ag2_r, fs2, fr2,
):
    p = lax.axis_index("pair")
    r = lax.axis_index("row")
    yh, z, c = r // 16, lax.rem(r // 2, 8), lax.rem(r, 2)
    chip = yh * 8 + z
    m = p // 2
    uc = lax.rem(m + 1, 2)
    half = lax.rem(m + p, 2)
    pu = jnp.where(p >= 2, p - 2, 1 - p)
    po = jnp.where(p <= 5, p + 2, 13 - p)
    partner = [jnp.where(uc == s, pu, po) for s in (0, 1)]
    mine = [jnp.where(uc == s, p == 0, p <= 6) for s in (0, 1)]
    lead = [jnp.where(uc == s, p != 1, p == 7) for s in (0, 1)]
    swap = jnp.logical_or(lax.rem(m, 2) == 1, p == 0)
    rows = x_hbm.shape[1]
    n_chunks = rows // CHUNK
    part = n_chunks // 2

    def chip_row(op, core):
        return lax.rem(yh + op[0], 2) * 16 + lax.rem(z + op[1], 8) * 2 + core

    def chip_index(op):
        return lax.rem(yh + op[0], 2) * 8 + lax.rem(z + op[1], 8)

    sibling = (p, chip_row((0, 0), 1 - c))
    peers = [(p, chip_row(op, c)) for op in CHIPS]

    def remote(src, dst, send, recv, device):
        return pltpu.make_async_remote_copy(
            src_ref=src, dst_ref=dst, send_sem=send, recv_sem=recv,
            device_id=device, device_id_type=MESH,
        )

    def load(k):
        return pltpu.make_async_copy(
            x_hbm.at[:, pl.ds(k * CHUNK, CHUNK)], xin.at[:, pl.ds(k * CHUNK, CHUNK)], lsem.at[k]
        )

    def early(n, s):
        src = pl.ds(pl.multiple_of((half * part + n) * CHUNK, CHUNK), CHUNK)
        dst = pl.ds(n * CHUNK, CHUNK)
        return remote(xin.at[:, src], ebuf.at[s, :, dst], es.at[s, n], er.at[s, n], (partner[s], r))

    for k in range(n_chunks):
        load(k).start()
    barrier = pltpu.get_barrier_semaphore()
    aside = sibling[1]
    near = jnp.where(c == 0, partner[0], partner[1])
    other = jnp.where(c == 0, partner[1], partner[0])
    everyone = [sibling] + peers + [(partner[0], r), (partner[1], r), (near, aside)]
    for device in everyone:
        pl.semaphore_signal(barrier, inc=1, device_id=device, device_id_type=MESH)

    def gram_chunk(k, g):
        load(k).wait()
        at = pl.ds(pl.multiple_of(k * CHUNK, CHUNK), CHUNK)
        high, low = split(jnp.concatenate([xin[0, at], xin[1, at]], 1))
        xhi[at] = high
        xlo[at] = low
        return g + mul(high, jnp.concatenate([high, low], 1), ((0,), (0,)))

    g = lax.fori_loop(0, n_chunks, gram_chunk, jnp.zeros((2 * BW, 4 * BW), F32))
    gl = g[:, 2 * BW:]
    g = g[:, :2 * BW] + (gl + gl.T)
    i, j = diag_mask()
    pay[0] = g[:BW, BW:]
    pay[1] = jnp.where(i >= j, g[:BW, :BW], g[BW:, BW:])
    low_diag = jnp.sum(jnp.where(i == j, g[BW:, BW:], 0.0), axis=0, keepdims=True)
    dl[...] = jnp.broadcast_to(low_diag, (8, BW))
    pl.semaphore_wait(barrier, len(everyone))

    c1 = remote(pay.at[1 - c], cbuf, cs.at[0], cr.at[0], sibling)
    c2 = remote(dl, dlr, cs.at[1], cr.at[1], sibling)
    c1.start()
    c2.start()
    c1.wait()
    c2.wait()
    rsrc[:, :8] = (pay[c] + cbuf[...]).reshape(16, 8, BW)
    rsrc[:, 8:] = jnp.broadcast_to((dl[...] + dlr[...])[None], (16, 8, BW))
    copies = []
    for n, op in enumerate(CHIPS):
        cp = remote(rsrc.at[chip_index(op)], rbuf.at[n], rs_s.at[n], rs_r.at[n], peers[n])
        cp.start()
        copies.append(cp)
    early(0, 0).start()
    early(0, 1).start()
    for cp in copies:
        cp.wait()
    total = rsrc[chip] + jnp.sum(rbuf[...], axis=0)
    low_diag = total[8:9]
    here = pl.ds(pl.multiple_of(chip * 8, 8), 8)
    res[here] = total[:8]
    copies = []
    for n, op in enumerate(CHIPS):
        cp = remote(res.at[here], res.at[here], ag_s.at[n], ag_r.at[n], peers[n])
        cp.start()
        copies.append(cp)
    early(1, 0).start()
    early(1, 1).start()
    for cp in copies:
        cp.wait()
    cp = remote(res, full.at[c], fs, fr, sibling)
    cp.start()
    for n in range(2, EARLY):
        early(n, 0).start()
        early(n, 1).start()
    full[c] = res[...]
    cp.wait()
    cross = full[0]
    packed = full[1]
    flipped = packed.T
    upper = jnp.where(i >= j, packed, flipped)
    lower = jnp.where(i == j, jnp.broadcast_to(low_diag, (BW, BW)), jnp.where(i < j, packed, flipped))
    up_diag = jnp.sum(jnp.where(i == j, upper, 0.0), axis=1, keepdims=True)
    [(h, v)] = rotations([(upper, lower, cross, up_diag, low_diag)])
    w = jnp.where(swap, jnp.concatenate([v[:, BW:], v[:, :BW]], 1), v)
    wh, wl = split(w)
    wbuf[0] = wh
    wbuf[1] = wl

    for s in (0, 1):
        wown[s] = w[:, s * BW:(s + 1) * BW]
    turns = [remote(wown.at[s], wfar.at[s], ws.at[s], wr.at[s], (partner[s], r)) for s in (0, 1)]
    for cp in turns:
        cp.start()

    def send(k, s):
        at = pl.ds(pl.multiple_of(k * CHUNK, CHUNK), CHUNK)
        return remote(own.at[s, at], far.at[s, at], ss.at[s, k], sr.at[s, k], (partner[s], r))

    def product(at):
        xh = xhi[at]
        dims = ((1,), (0,))
        y = mul(xh, wbuf[0], dims) + (mul(xh, wbuf[1], dims) + mul(xlo[at], wbuf[0], dims))
        yh, yl = split(y)
        for s in (0, 1):
            cols = slice(s * BW, (s + 1) * BW)
            own[s, at] = y[:, cols]
            bhi[s, at, :BW] = yh[:, cols]
            blo[s, at, :BW] = yl[:, cols]

    def rows_at(begin, count):
        return pl.ds(pl.multiple_of(begin * CHUNK, CHUNK), count * CHUNK)

    def first_part(n, carry):
        k = half * part + n
        product(rows_at(k, 1))
        send(k, 0).start()
        send(k, 1).start()
        return carry

    lax.fori_loop(EARLY, part, first_part, 0)

    hw = small(h, w)
    for s in (0, 1):
        gown[s] = small(w[:, s * BW:(s + 1) * BW].T, hw[:, s * BW:(s + 1) * BW])

    grams = [remote(gown.at[s], gfar.at[s], gs.at[s], gr.at[s], (partner[s], r)) for s in (0, 1)]
    for cp in grams:
        cp.start()

    def second_product(n, carry):
        product(rows_at((1 - half) * part + n * (part // 2), part // 2))
        return carry

    lax.fori_loop(0, 2, second_product, 0)
    product(rows_at(half * part, EARLY))

    def cross(k, acc):
        at = pl.ds(pl.multiple_of(k * CHUNK, CHUNK), CHUNK)
        out_acc = []
        for s in (0, 1):
            lh, ll = bhi[s, at, :BW], blo[s, at, :BW]
            fh, fl = split(far[s, at])
            bhi[s, at, BW:] = fh
            blo[s, at, BW:] = fl
            dims = ((0,), (0,))
            q = mul(lh, jnp.concatenate([fh, fl], 1), dims)
            out_acc.append(acc[s] + (q[:, :BW] + (q[:, BW:] + mul(ll, fh, dims))))
        return tuple(out_acc)

    for cp in turns:
        cp.wait_recv()
    wparts = []
    for s in (0, 1):
        fh, fl = split(wfar[s])
        wparts.append((fh, jnp.concatenate([fh, fl], 1)))

    def early_chunk(n, acc):
        k = (1 - half) * part + n
        at = pl.ds(pl.multiple_of(k * CHUNK, CHUNK), CHUNK)
        came = pl.ds(pl.multiple_of(n * CHUNK, CHUNK), CHUNK)
        dims = ((1,), (0,))
        for s in (0, 1):
            early(n, s).wait_recv()
            eh, el = split(jnp.concatenate([ebuf[s, 0, came], ebuf[s, 1, came]], 1))
            q = mul(eh, wparts[s][1], dims)
            far[s, at] = q[:, :BW] + (q[:, BW:] + mul(el, wparts[s][0], dims))
        return cross(k, acc)

    def cross_chunk(n, acc):
        k = (1 - half) * part + n
        send(k, 0).wait_recv()
        send(k, 1).wait_recv()
        return cross(k, acc)

    zero = jnp.zeros((BW, BW), F32)
    acc = lax.fori_loop(0, EARLY, early_chunk, (zero, zero))
    acc = lax.fori_loop(EARLY, part, cross_chunk, acc)

    def first_wait(n, carry):
        send(half * part + n, 0).wait_send()
        send(half * part + n, 1).wait_send()
        return carry

    def early_wait(n, carry):
        early(n, 0).wait_send()
        early(n, 1).wait_send()
        return carry

    lax.fori_loop(EARLY, part, first_wait, 0)
    lax.fori_loop(0, EARLY, early_wait, 0)
    for cp in turns:
        cp.wait_send()
    for s in (0, 1):
        pay2[s] = jnp.where(mine[s], acc[s], acc[s].T)
    copies = [
        remote(pay2.at[c], cbuf2.at[0], cs2.at[0], cr2.at[0], (near, r)),
        remote(pay2.at[1 - c], cbuf2.at[1], cs2.at[1], cr2.at[1], (other, aside)),
        remote(pay2.at[1 - c], cbuf2.at[2], cs2.at[2], cr2.at[2], sibling),
    ]
    for cp in copies:
        cp.start()

    def second_start(step):
        begin = sum(PACE[:step])
        for n in range(begin, begin + PACE[step]):
            k = (1 - half) * part + n
            send(k, 0).start()
            send(k, 1).start()

    second_start(0)
    for cp in copies:
        cp.wait()
    acc2[...] = (pay2[c] + cbuf2[2]) + (cbuf2[0] + cbuf2[1])
    copies = []
    for n, op in enumerate(CHIPS):
        at = pl.ds(pl.multiple_of(chip_index(op) * 8, 8), 8)
        cp = remote(acc2.at[at], rbuf2.at[n], rs2_s.at[n], rs2_r.at[n], peers[n])
        cp.start()
        copies.append(cp)
    second_start(1)
    for cp in copies:
        cp.wait()
    res2[here] = acc2[here] + jnp.sum(rbuf2[...], axis=0)
    copies = []
    for n, op in enumerate(CHIPS):
        cp = remote(res2.at[here], res2.at[here], ag2_s.at[n], ag2_r.at[n], peers[n])
        cp.start()
        copies.append(cp)
    second_start(2)
    for cp in copies:
        cp.wait()
    cp = remote(res2, full2.at[c], fs2, fr2, sibling)
    cp.start()
    second_start(3)
    full2[c] = res2[...]
    for q in grams:
        q.wait()
    cp.wait()

    items = []
    for s in (0, 1):
        first = jnp.where(mine[s], gown[s], gfar[s])
        second = jnp.where(mine[s], gfar[s], gown[s])
        fd = jnp.sum(jnp.where(i == j, first, 0.0), axis=1, keepdims=True)
        sd = jnp.sum(jnp.where(i == j, second, 0.0), axis=0, keepdims=True)
        items.append((first, second, full2[s], fd, sd))
    weights = []
    for s, (_, v) in enumerate(rotations(items)):
        v = jnp.where(lead[s], v[:, :BW], v[:, BW:])
        v = jnp.where(mine[s], v, jnp.concatenate([v[BW:], v[:BW]], 0))
        vh, vl = split(v)
        weights.append((vh, jnp.concatenate([vh, vl], 1)))

    def store(begin, count, s):
        at = rows_at(begin, count)
        slot = jnp.where(uc == s, 0, 1)
        return pltpu.make_async_copy(out.at[s, at], o_hbm.at[slot, at], osem.at[s, begin])

    def last_product(begin, count):
        at = rows_at(begin, count)
        dims = ((1,), (0,))
        for s in (0, 1):
            vh, vhl = weights[s]
            q = mul(bhi[s, at], vhl, dims)
            out[s, at] = q[:, :BW] + (q[:, BW:] + mul(blo[s, at], vh, dims))
            store(begin, count, s).start()

    def last_a(n, carry):
        last_product((1 - half) * part + n * (part // 2), part // 2)
        return carry

    lax.fori_loop(0, 2, last_a, 0)

    def last_b(n, carry):
        begin = half * part + n * LAST
        at = rows_at(begin, LAST)
        for k in range(LAST):
            send(begin + k, 0).wait_recv()
            send(begin + k, 1).wait_recv()
        for s in (0, 1):
            fh, fl = split(far[s, at])
            bhi[s, at, BW:] = fh
            blo[s, at, BW:] = fl
        last_product(begin, LAST)
        return carry

    lax.fori_loop(0, part // LAST, last_b, 0)

    def finish_a(n, carry):
        for s in (0, 1):
            store((1 - half) * part + n * (part // 2), part // 2, s).wait()
        return carry

    def finish_b(n, carry):
        for s in (0, 1):
            store(half * part + n * LAST, LAST, s).wait()
        return carry

    lax.fori_loop(0, 2, finish_a, 0)
    lax.fori_loop(0, part // LAST, finish_b, 0)

    def finish_send(n, carry):
        k = (1 - half) * part + n
        send(k, 0).wait_send()
        send(k, 1).wait_send()
        return carry

    lax.fori_loop(0, part, finish_send, 0)


def body(matrix):
    rows = matrix.shape[1]
    n_chunks = rows // CHUNK
    dma = pltpu.SemaphoreType.DMA
    n = len(CHIPS)
    block = pltpu.VMEM((2, rows, BW), F32)
    square = pltpu.VMEM((BW, BW), F32)
    squares = pltpu.VMEM((2, BW, BW), F32)
    tile = pltpu.VMEM((8, BW), F32)
    scratch = [
        block, pltpu.VMEM((rows, 2 * BW), BF16), pltpu.VMEM((rows, 2 * BW), BF16), block, block, block,
        pltpu.VMEM((2, rows, 2 * BW), BF16), pltpu.VMEM((2, rows, 2 * BW), BF16),
        squares, square, tile, tile, pltpu.VMEM((16, 16, BW), F32), pltpu.VMEM((n, 16, BW), F32),
        square, squares, pltpu.VMEM((2, 2 * BW, 2 * BW), BF16),
        pltpu.VMEM((2, 2, EARLY * CHUNK, BW), F32), pltpu.VMEM((2, 2 * BW, BW), F32), pltpu.VMEM((2, 2 * BW, BW), F32),
        squares, squares, squares, pltpu.VMEM((3, BW, BW), F32), square, pltpu.VMEM((n, 8, BW), F32), square, squares,
        dma((n_chunks,)), dma((2, n_chunks)), dma((2,)), dma((2,)), dma((n,)), dma((n,)), dma((n,)), dma((n,)),
        dma, dma, dma((2, EARLY)), dma((2, EARLY)), dma((2,)), dma((2,)),
        dma((2, n_chunks)), dma((2, n_chunks)), dma((2,)), dma((2,)), dma((3,)), dma((3,)),
        dma((n,)), dma((n,)), dma((n,)), dma((n,)), dma, dma,
    ]
    return pl.pallas_call(
        kernel,
        out_shape=jax.ShapeDtypeStruct(matrix.shape, F32),
        in_specs=[pl.BlockSpec(memory_space=pl.ANY)],
        out_specs=pl.BlockSpec(memory_space=pl.ANY),
        scratch_shapes=scratch,
        compiler_params=pltpu.CompilerParams(
            collective_id=0, has_side_effects=True, vmem_limit_bytes=48 << 20
        ),
    )(matrix)


def solution(mesh):
    specs = P(None, "row", "pair")
    return jax.shard_map(body, mesh=mesh, in_specs=(specs,), out_specs=specs, check_vma=False)
```

time: 114 us -> 83.6 us (0.73)
  Pallas kernels: 112 us -> 81.5 us
    pallas_call x1, Pallas kernels: 112 us -> 81.5 us  [body(): pl.pallas_call(kernel, out_shape=jax.ShapeDtypeStruct(matrix.shape, F32),...]
where the time goes in v2:
time: 83.6 us; the launch traced here: 83.5 us
  Pallas kernels  81.5 us (97%)
  local copies, waits for them, and re-layouts  2.02 us (2%)
    pallas_call x1, Pallas kernels, body(): pl.pallas_call(kernel, out_shape=jax.ShapeDtypeStruct(matrix.shape, F32),...  81.5 us
    unnamed x1, local copies, waits for them, and re-layouts  2.02 us

profile of v2, /device:TPU:1, one launch (start us, length us, event | category | flops | bytes accessed | tf_op | source)
XLA Modules:
  0.0 83.5 jit_solution(11492242366461139525)
XLA Ops:
  0.0 81.5 %shard_map.17 = f32[2,4096,128]{2,1,0:T(8,128)S(1)} custom-call(f32[2,4096,128]{2,1,0:T(8,128)} %x_hbm.1), custom_call_target="tpu_custom_call" | custom-call | tf_op jit(solution)/shard_map/pallas_call | solution.py:477
  81.5 2.0 %copy.3 = f32[2,4096,128]{2,1,0:T(8,128)} copy(f32[2,4096,128]{2,1,0:T(8,128)S(1)} %shard_map.17) | data formatting | bytes 8388608

commit v3 on v2

--- a/solution.py
+++ b/solution.py
@@ -10,7 +10,8 @@
 BW = 128
 CHUNK = 256
 EARLY = 3
-PACE = (1, 2, 2, 3)
+PACE = (1, 1, 2, 3, 1)
+LEAD = 2
 LAST = 2
 MESH = pl.DeviceIdType.MESH
 F32 = jnp.float32
@@ -40,7 +41,7 @@
     )
 
 
-small = mul6
+small = mul3
 
 
 def diag_mask():
@@ -105,12 +106,12 @@
 
 
 def kernel(
-    x_hbm, o_hbm,
-    xin, xhi, xlo, own, far, out, bhi, blo,
+    x_hbm, o_ref,
+    xin, xhi, xlo, own, far, bhi, blo,
     pay, cbuf, dl, dlr, rsrc, rbuf, res, full, wbuf,
     ebuf, wown, wfar, gown, gfar, pay2, cbuf2, acc2, rbuf2, res2, full2,
-    lsem, osem, cs, cr, rs_s, rs_r, ag_s, ag_r, fs, fr,
-    es, er, ws, wr, ss, sr, gs, gr, cs2, cr2, rs2_s, rs2_r, ag2_s, ag2_r, fs2, fr2,
+    lsem, cs, cr, rs_s, rs_r, ag_s, ag_r, fs, fr,
+    es, er, ws, wr, ws2, wr2, ss, sr, gs, gr, gs2, gr2, cs2, cr2, rs2_s, rs2_r, ag2_s, ag2_r, fs2, fr2,
 ):
     p = lax.axis_index("pair")
     r = lax.axis_index("row")
@@ -233,7 +234,14 @@
 
     for s in (0, 1):
         wown[s] = w[:, s * BW:(s + 1) * BW]
-    turns = [remote(wown.at[s], wfar.at[s], ws.at[s], wr.at[s], (partner[s], r)) for s in (0, 1)]
+    wpart = pl.ds(pl.multiple_of(c * BW, BW), BW)
+    turns = [
+        remote(wown.at[s, wpart], wfar.at[s, wpart], ws.at[s], wr.at[s], (partner[s], r))
+        for s in (0, 1)
+    ]
+    passed = [
+        remote(wfar.at[s, wpart], wfar.at[s, wpart], ws2.at[s], wr2.at[s], sibling) for s in (0, 1)
+    ]
     for cp in turns:
         cp.start()
 
@@ -262,13 +270,24 @@
         send(k, 1).start()
         return carry
 
-    lax.fori_loop(EARLY, part, first_part, 0)
+    lax.fori_loop(EARLY, EARLY + LEAD, first_part, 0)
+    for s in (0, 1):
+        turns[s].wait_recv()
+        passed[s].start()
+    lax.fori_loop(EARLY + LEAD, part, first_part, 0)
 
     hw = small(h, w)
     for s in (0, 1):
         gown[s] = small(w[:, s * BW:(s + 1) * BW].T, hw[:, s * BW:(s + 1) * BW])
 
-    grams = [remote(gown.at[s], gfar.at[s], gs.at[s], gr.at[s], (partner[s], r)) for s in (0, 1)]
+    gpart = pl.ds(pl.multiple_of(c * (BW // 2), BW // 2), BW // 2)
+    grams = [
+        remote(gown.at[s, gpart], gfar.at[s, gpart], gs.at[s], gr.at[s], (partner[s], r))
+        for s in (0, 1)
+    ]
+    grams_passed = [
+        remote(gfar.at[s, gpart], gfar.at[s, gpart], gs2.at[s], gr2.at[s], sibling) for s in (0, 1)
+    ]
     for cp in grams:
         cp.start()
 
@@ -277,6 +296,15 @@
         return carry
 
     lax.fori_loop(0, 2, second_product, 0)
+
+    def second_start(step):
+        begin = sum(PACE[:step])
+        for n in range(begin, begin + PACE[step]):
+            k = (1 - half) * part + n
+            send(k, 0).start()
+            send(k, 1).start()
+
+    second_start(0)
     product(rows_at(half * part, EARLY))
 
     def cross(k, acc):
@@ -292,7 +320,7 @@
             out_acc.append(acc[s] + (q[:, :BW] + (q[:, BW:] + mul(ll, fh, dims))))
         return tuple(out_acc)
 
-    for cp in turns:
+    for cp in passed:
         cp.wait_recv()
     wparts = []
     for s in (0, 1):
@@ -333,7 +361,7 @@
 
     lax.fori_loop(EARLY, part, first_wait, 0)
     lax.fori_loop(0, EARLY, early_wait, 0)
-    for cp in turns:
+    for cp in turns + passed:
         cp.wait_send()
     for s in (0, 1):
         pay2[s] = jnp.where(mine[s], acc[s], acc[s].T)
@@ -345,14 +373,7 @@
     for cp in copies:
         cp.start()
 
-    def second_start(step):
-        begin = sum(PACE[:step])
-        for n in range(begin, begin + PACE[step]):
-            k = (1 - half) * part + n
-            send(k, 0).start()
-            send(k, 1).start()
-
-    second_start(0)
+    second_start(1)
     for cp in copies:
         cp.wait()
     acc2[...] = (pay2[c] + cbuf2[2]) + (cbuf2[0] + cbuf2[1])
@@ -362,7 +383,10 @@
         cp = remote(acc2.at[at], rbuf2.at[n], rs2_s.at[n], rs2_r.at[n], peers[n])
         cp.start()
         copies.append(cp)
-    second_start(1)
+    for s in (0, 1):
+        grams[s].wait_recv()
+        grams_passed[s].start()
+    second_start(2)
     for cp in copies:
         cp.wait()
     res2[here] = acc2[here] + jnp.sum(rbuf2[...], axis=0)
@@ -371,14 +395,16 @@
         cp = remote(res2.at[here], res2.at[here], ag2_s.at[n], ag2_r.at[n], peers[n])
         cp.start()
         copies.append(cp)
-    second_start(2)
+    second_start(3)
     for cp in copies:
         cp.wait()
     cp = remote(res2, full2.at[c], fs2, fr2, sibling)
     cp.start()
-    second_start(3)
+    second_start(4)
     full2[c] = res2[...]
     for q in grams:
+        q.wait_send()
+    for q in grams_passed:
         q.wait()
     cp.wait()
 
@@ -396,19 +422,13 @@
         vh, vl = split(v)
         weights.append((vh, jnp.concatenate([vh, vl], 1)))
 
-    def store(begin, count, s):
-        at = rows_at(begin, count)
-        slot = jnp.where(uc == s, 0, 1)
-        return pltpu.make_async_copy(out.at[s, at], o_hbm.at[slot, at], osem.at[s, begin])
-
     def last_product(begin, count):
         at = rows_at(begin, count)
         dims = ((1,), (0,))
         for s in (0, 1):
             vh, vhl = weights[s]
             q = mul(bhi[s, at], vhl, dims)
-            out[s, at] = q[:, :BW] + (q[:, BW:] + mul(blo[s, at], vh, dims))
-            store(begin, count, s).start()
+            o_ref[jnp.where(uc == s, 0, 1), at] = q[:, :BW] + (q[:, BW:] + mul(blo[s, at], vh, dims))
 
     def last_a(n, carry):
         last_product((1 - half) * part + n * (part // 2), part // 2)
@@ -431,19 +451,6 @@
 
     lax.fori_loop(0, part // LAST, last_b, 0)
 
-    def finish_a(n, carry):
-        for s in (0, 1):
-            store((1 - half) * part + n * (part // 2), part // 2, s).wait()
-        return carry
-
-    def finish_b(n, carry):
-        for s in (0, 1):
-            store(half * part + n * LAST, LAST, s).wait()
-        return carry
-
-    lax.fori_loop(0, 2, finish_a, 0)
-    lax.fori_loop(0, part // LAST, finish_b, 0)
-
     def finish_send(n, carry):
         k = (1 - half) * part + n
         send(k, 0).wait_send()
@@ -463,22 +470,23 @@
     squares = pltpu.VMEM((2, BW, BW), F32)
     tile = pltpu.VMEM((8, BW), F32)
     scratch = [
-        block, pltpu.VMEM((rows, 2 * BW), BF16), pltpu.VMEM((rows, 2 * BW), BF16), block, block, block,
+        block, pltpu.VMEM((rows, 2 * BW), BF16), pltpu.VMEM((rows, 2 * BW), BF16), block, block,
         pltpu.VMEM((2, rows, 2 * BW), BF16), pltpu.VMEM((2, rows, 2 * BW), BF16),
         squares, square, tile, tile, pltpu.VMEM((16, 16, BW), F32), pltpu.VMEM((n, 16, BW), F32),
         square, squares, pltpu.VMEM((2, 2 * BW, 2 * BW), BF16),
         pltpu.VMEM((2, 2, EARLY * CHUNK, BW), F32), pltpu.VMEM((2, 2 * BW, BW), F32), pltpu.VMEM((2, 2 * BW, BW), F32),
         squares, squares, squares, pltpu.VMEM((3, BW, BW), F32), square, pltpu.VMEM((n, 8, BW), F32), square, squares,
-        dma((n_chunks,)), dma((2, n_chunks)), dma((2,)), dma((2,)), dma((n,)), dma((n,)), dma((n,)), dma((n,)),
-        dma, dma, dma((2, EARLY)), dma((2, EARLY)), dma((2,)), dma((2,)),
-        dma((2, n_chunks)), dma((2, n_chunks)), dma((2,)), dma((2,)), dma((3,)), dma((3,)),
+        dma((n_chunks,)), dma((2,)), dma((2,)), dma((n,)), dma((n,)), dma((n,)), dma((n,)),
+        dma, dma, dma((2, EARLY)), dma((2, EARLY)), dma((2,)), dma((2,)), dma((2,)), dma((2,)),
+        dma((2, n_chunks)), dma((2, n_chunks)), dma((2,)), dma((2,)), dma((2,)), dma((2,)),
+        dma((3,)), dma((3,)),
         dma((n,)), dma((n,)), dma((n,)), dma((n,)), dma, dma,
     ]
     return pl.pallas_call(
         kernel,
         out_shape=jax.ShapeDtypeStruct(matrix.shape, F32),
         in_specs=[pl.BlockSpec(memory_space=pl.ANY)],
-        out_specs=pl.BlockSpec(memory_space=pl.ANY),
+        out_specs=pl.BlockSpec(memory_space=pltpu.VMEM),
         scratch_shapes=scratch,
         compiler_params=pltpu.CompilerParams(
             collective_id=0, has_side_effects=True, vmem_limit_bytes=48 << 20

time: 83.6 us -> 78.9 us (0.944)
  Pallas kernels: 81.5 us -> 76.8 us
    pallas_call x1, Pallas kernels: 81.5 us -> 76.8 us  [body(): pl.pallas_call(kernel, out_shape=jax.ShapeDtypeStruct(matrix.shape, F32),...]
where the time goes in v3:
time: 78.9 us
  Pallas kernels  76.8 us (97%)
  local copies, waits for them, and re-layouts  2.02 us (3%)
    pallas_call x1, Pallas kernels, body(): pl.pallas_call(kernel, out_shape=jax.ShapeDtypeStruct(matrix.shape, F32),...  76.8 us
    unnamed x1, local copies, waits for them, and re-layouts  2.02 us

profile of v3, /device:TPU:1, one launch (start us, length us, event | category | flops | bytes accessed | tf_op | source)
XLA Modules:
  0.0 78.9 jit_solution(10254272134109245524)
XLA Ops:
  0.0 76.8 %shard_map.17 = f32[2,4096,128]{2,1,0:T(8,128)S(1)} custom-call(f32[2,4096,128]{2,1,0:T(8,128)} %x_hbm.1), custom_call_target="tpu_custom_call" | custom-call | tf_op jit(solution)/shard_map/pallas_call | solution.py:485
  76.8 2.0 %copy.3 = f32[2,4096,128]{2,1,0:T(8,128)} copy(f32[2,4096,128]{2,1,0:T(8,128)S(1)} %shard_map.17) | data formatting | bytes 8388608

commit v4 on v3

--- a/solution.py
+++ b/solution.py
@@ -11,7 +11,7 @@
 CHUNK = 256
 EARLY = 3
 PACE = (1, 1, 2, 3, 1)
-LEAD = 2
+LEAD = 1
 LAST = 2
 MESH = pl.DeviceIdType.MESH
 F32 = jnp.float32

time: 78.9 us -> 78.9 us (level)
  no operation moved by 1% of the time
where the time goes in v4:
time: 78.9 us; the launch traced here: 78.8 us
  Pallas kernels  76.8 us (97%)
  local copies, waits for them, and re-layouts  2.02 us (3%)
    pallas_call x1, Pallas kernels, body(): pl.pallas_call(kernel, out_shape=jax.ShapeDtypeStruct(matrix.shape, F32),...  76.8 us
    unnamed x1, local copies, waits for them, and re-layouts  2.02 us

profile of v4, /device:TPU:1, one launch (start us, length us, event | category | flops | bytes accessed | tf_op | source)
XLA Modules:
  0.0 78.8 jit_solution(16494204835781975777)
XLA Ops:
  0.0 76.8 %shard_map.17 = f32[2,4096,128]{2,1,0:T(8,128)S(1)} custom-call(f32[2,4096,128]{2,1,0:T(8,128)} %x_hbm.1), custom_call_target="tpu_custom_call" | custom-call | tf_op jit(solution)/shard_map/pallas_call | solution.py:485
  76.8 2.0 %copy.3 = f32[2,4096,128]{2,1,0:T(8,128)} copy(f32[2,4096,128]{2,1,0:T(8,128)S(1)} %shard_map.17) | data formatting | bytes 8388608
